TPU v7x, 32 devices: a whole 2x2x4 slice. The times are simulated.
32 devices in a mesh: groups: 2 (over x), fsdp: 16 (over z, y, core).
Axes of the slice: x: 2, y: 2, z: 4, core: 2. Of those that a mesh axis runs over, the one named last changes fastest.
Arguments:
- layer_input: bfloat16 [512, 8192], P('groups', 'fsdp'), parts along dimension 0, may hold values from -6 to 6
- norm_gain: bfloat16 [8192], P('fsdp'), may hold values from 0.099609375 to 1.8984375
- w_query: bfloat16 [8192, 8192], P(None, 'fsdp'), may hold values from -0.0625 to 0.0625
- w_key: bfloat16 [8192, 1024], P('fsdp'), may hold values from -0.09375 to 0.09375
- w_value: bfloat16 [8192, 1024], P('fsdp'), may hold values from -0.09375 to 0.09375
- w_out: bfloat16 [8192, 8192], P('fsdp'), may hold values from -0.0625 to 0.0625
- cart_key: bfloat16 [4096, 1024], P(('groups', 'fsdp')), parts along dimension 0, may hold values from -100 to 100
- cart_value: bfloat16 [4096, 1024], P(('groups', 'fsdp')), parts along dimension 0, may hold values from -6 to 6
- grad_out: bfloat16 [512, 8192], P('groups', 'fsdp'), parts along dimension 0, may hold values from -6 to 6
Outputs:
- attn_out: bfloat16 [512, 8192], P('groups', 'fsdp'), parts along dimension 0
- grad_key: float32 [4096, 1024], P(('groups', 'fsdp')), parts along dimension 0
- grad_value: float32 [4096, 1024], P(('groups', 'fsdp')), parts along dimension 0
- new_keys: bfloat16 [512, 1024], P('groups', 'fsdp'), parts along dimension 0
- new_values: bfloat16 [512, 1024], P('groups', 'fsdp'), parts along dimension 0
There are 2 independent parts, one for each index of `groups`. A program takes and returns all parts, laid end to end along the dimension named above; an argument that names none is the same for every part. Nothing has to cross between parts.
All inputs are finite; a program needn't handle non-finite values.
Results may differ from a plain program's by a relative error of at most 0.015.
The roundings to bfloat16 on the way count: a program that leaves them out, or rounds other values in their place, can miss the bound.
Values may be sent and summed in bfloat16 or wider, within the bound.
A program may use at most 128 MiB of HBM per device.

v0:
```python
import jax
import jax.numpy as jnp
from jax import lax
from jax.sharding import PartitionSpec as P

H = 64
KV = 8
HD = 128
C = 2048
SEQ = 64


def rotate(vectors, positions):
    half_dim = vectors.shape[-1] // 2
    frequency = jnp.exp(
        -jnp.log(500000.0) * jnp.arange(half_dim, dtype=jnp.float32) * (2.0 / vectors.shape[-1])
    )
    angles = positions.astype(jnp.float32)[:, None] * frequency[None, :]
    cosines = jnp.cos(angles)[:, None, :]
    sine_table = jnp.sin(angles)[:, None, :]
    first_half = vectors[..., :half_dim]
    second = vectors[..., half_dim:]
    return jnp.concatenate(
        [first_half * cosines - second * sine_table, second * cosines + first_half * sine_table], -1
    )


def head_block(queries, slot_keys, slot_values, token_keys, token_values, grad_heads, seq_len):
    scaling = queries.shape[-1] ** (-0.5)
    token_count = queries.shape[1]
    score_cart = (
        jnp.einsum("gtd,cd->gtc", queries, slot_keys, preferred_element_type=jnp.float32) * scaling
    )
    score_tok = (
        jnp.einsum("gtd,sd->gts", queries, token_keys, preferred_element_type=jnp.float32) * scaling
    )
    index_rows = jnp.arange(token_count)
    causal = (index_rows[:, None] // seq_len == index_rows[None, :] // seq_len) & (
        index_rows[None, :] <= index_rows[:, None]
    )
    score_tok = jnp.where(causal[None], score_tok, -jnp.inf)
    row_max = jnp.maximum(
        jnp.max(score_cart, -1, keepdims=True), jnp.max(score_tok, -1, keepdims=True)
    )
    exp_cart = jnp.exp(score_cart - row_max)
    exp_tok = jnp.exp(score_tok - row_max)
    totals = jnp.sum(exp_cart, -1, keepdims=True) + jnp.sum(exp_tok, -1, keepdims=True)
    prob_cart = exp_cart / totals
    rounded_cart = prob_cart.astype(jnp.bfloat16)
    rounded_tok = (exp_tok / totals).astype(jnp.bfloat16)
    mixture = jnp.einsum(
        "gtc,cd->gtd", rounded_cart, slot_values, preferred_element_type=jnp.float32
    )
    mixture = mixture + jnp.einsum(
        "gts,sd->gtd", rounded_tok, token_values, preferred_element_type=jnp.float32
    )
    outputs = mixture.astype(jnp.bfloat16)
    grad_prob_cart = jnp.einsum(
        "gtd,cd->gtc", grad_heads, slot_values, preferred_element_type=jnp.float32
    )
    deltas = jnp.sum(
        grad_heads.astype(jnp.float32) * outputs.astype(jnp.float32), -1, keepdims=True
    )
    grad_score = (prob_cart * (grad_prob_cart - deltas)).astype(jnp.bfloat16)
    grad_keys = (
        jnp.einsum("gtc,gtd->cd", grad_score, queries, preferred_element_type=jnp.float32) * scaling
    )
    grad_values = jnp.einsum(
        "gtc,gtd->cd", rounded_cart, grad_heads, preferred_element_type=jnp.float32
    )
    return (outputs, grad_keys, grad_values)


def on_device(
    layer_input, norm_gain, w_query, w_key, w_value, w_out, cart_key, cart_value, grad_out
):
    devices = lax.axis_size("fsdp")
    my_index = lax.axis_index("fsdp")
    token_count = layer_input.shape[0]
    feature_count = layer_input.shape[1]
    local_heads = w_query.shape[1] // HD
    slot_count = cart_key.shape[0]
    kv_width = w_key.shape[1]
    gathered, gathered_gain = (
        lax.all_gather(layer_input, "fsdp", axis=1, tiled=True),
        lax.all_gather(norm_gain, "fsdp", axis=0, tiled=True),
    )
    gathered_f32 = gathered.astype(jnp.float32)
    inverse_rms = lax.rsqrt(jnp.mean(gathered_f32 * gathered_f32, -1, keepdims=True) + 1e-05)
    normed = (gathered_f32 * inverse_rms * gathered_gain.astype(jnp.float32)[None, :]).astype(
        jnp.bfloat16
    )
    own_part = lax.dynamic_slice_in_dim(normed, my_index * feature_count, feature_count, 1)
    partial_kv = jnp.concatenate(
        [
            jnp.dot(own_part, w_key, preferred_element_type=jnp.float32),
            jnp.dot(own_part, w_value, preferred_element_type=jnp.float32),
        ],
        1,
    )
    token_kv = lax.psum(partial_kv, "fsdp")
    positions = C + jnp.arange(token_count) % SEQ
    all_token_keys = (
        rotate(token_kv[:, :kv_width].reshape(token_count, kv_width // HD, HD), positions)
        .reshape(token_count, kv_width)
        .astype(jnp.bfloat16)
    )
    all_token_values = token_kv[:, kv_width:].astype(jnp.bfloat16)
    column_count = kv_width // devices
    new_keys = lax.dynamic_slice_in_dim(all_token_keys, my_index * column_count, column_count, 1)
    new_values = lax.dynamic_slice_in_dim(
        all_token_values, my_index * column_count, column_count, 1
    )
    kv_group = my_index * local_heads // (H // KV)
    token_keys = lax.dynamic_slice_in_dim(all_token_keys, kv_group * HD, HD, 1)
    token_values = lax.dynamic_slice_in_dim(all_token_values, kv_group * HD, HD, 1)
    queries = jnp.dot(normed, w_query, preferred_element_type=jnp.float32).reshape(
        token_count, local_heads, HD
    )
    queries = rotate(queries, positions).astype(jnp.bfloat16).transpose(1, 0, 2)
    spread_keys = jnp.repeat(cart_key.reshape(slot_count, KV, HD), devices // KV, axis=1)
    spread_values = jnp.repeat(cart_value.reshape(slot_count, KV, HD), devices // KV, axis=1)
    own_slots = lax.all_to_all(
        jnp.concatenate([spread_keys, spread_values], 2),
        "fsdp",
        split_axis=1,
        concat_axis=0,
        tiled=True,
    )
    slot_keys = own_slots[:, 0, :HD]
    slot_values = own_slots[:, 0, HD:]
    cotangent = lax.all_gather(grad_out, "fsdp", axis=1, tiled=True)
    grad_heads = lax.dot_general(
        cotangent, w_out, (((1,), (1,)), ((), ())), preferred_element_type=jnp.float32
    )
    grad_heads = (
        grad_heads.astype(jnp.bfloat16).reshape(token_count, local_heads, HD).transpose(1, 0, 2)
    )
    outputs, grad_keys, grad_values = head_block(
        queries, slot_keys, slot_values, token_keys, token_values, grad_heads, SEQ
    )
    head_outputs = outputs.transpose(1, 0, 2).reshape(token_count, local_heads * HD)
    partial_out = jnp.dot(head_outputs, w_out, preferred_element_type=jnp.float32)
    attn_out = lax.psum_scatter(partial_out, "fsdp", scatter_dimension=1, tiled=True).astype(
        jnp.bfloat16
    )
    total_slots = grad_keys.shape[0]
    stacked = jnp.concatenate([grad_keys, grad_values], 1).reshape(
        devices, total_slots // devices, 2 * HD
    )
    received = lax.all_to_all(stacked, "fsdp", split_axis=0, concat_axis=0, tiled=True)
    summed = jnp.sum(
        received.reshape(KV, devices // KV, total_slots // devices, 2 * HD), axis=1
    ).transpose(1, 0, 2)
    grad_key = summed[:, :, :HD].reshape(total_slots // devices, KV * HD)
    grad_value = summed[:, :, HD:].reshape(total_slots // devices, KV * HD)
    return (attn_out, grad_key, grad_value, new_keys, new_values)


def solution(mesh):
    return jax.shard_map(
        on_device,
        mesh=mesh,
        in_specs=(
            P("groups", "fsdp"),
            P("fsdp"),
            P(None, "fsdp"),
            P("fsdp", None),
            P("fsdp", None),
            P("fsdp", None),
            P(("groups", "fsdp"), None),
            P(("groups", "fsdp"), None),
            P("groups", "fsdp"),
        ),
        out_specs=(
            P("groups", "fsdp"),
            P(("groups", "fsdp"), None),
            P(("groups", "fsdp"), None),
            P("groups", "fsdp"),
            P("groups", "fsdp"),
        ),
        check_vma=False,
    )
```

profile of v0, /device:TPU:0, one launch (start us, length us, event | category | flops | bytes accessed | tf_op | source)
XLA Modules:
  0.0 399.3 jit_solution(2381138714927701704)
XLA Ops:
  7.2 0.7 all-gather.4.cloned.1.call-update
  8.0 0.7 all-gather.6.cloned.1.call-update
  8.7 1.0 copy_bitcast_fusion.4
  9.7 1.0 copy_bitcast_fusion.3
  10.9 1.1 pad_maximum_fusion.1
  12.0 7.4 %all-to-all-start = ((bf16[128,16,256]{2,0,1:T(8,128)(2,1)}), bf16[128,16,256]{2,0,1:T(8,128)(2,1)S(1)}, u32[]{:S(2)}, u32[]{:S(2)}) async-start(bf16[128,16,256]{2,0,1:T(8,128)(2,1)} %pad_maximum_fusion.1), calls=%async_computation | async-start | bytes 2097152 | tf_op jit(solution)/shard_map/all_to_all | solution.py:123
  19.4 0.7 reshape.259
  20.1 40.6 %all-gather = bf16[16,1,512]{2,1,0:T(2,128)(2,1)S(1)} all-gather(bf16[1,1,512]{2,1,0:T(2,128)(2,1)S(1)} %reshape.259), channel_id=1, replica_groups=mesh['groups'=2,'fsdp'=16] {'fsdp'}, dimensions={0}, use_global_device_ids=true | all-gather | bytes 17408 | tf_op jit(solution)/shard_map/all_gather | solution.py:86
  60.9 0.5 multiply_cosine_fusion
  61.4 17.4 %all-gather.4.cloned.1.call-done = bf16[256,8192]{1,0:T(8,128)(2,1)} async-done(((bf16[256,512]{1,0:T(8,128)(2,1)}), bf16[256,8192]{1,0:T(8,128)(2,1)}) %all-gather.4.cloned.1.call-update) | async-done | bytes 4194320 | tf_op jit(solution)/shard_map/all_gather | solution.py:85
  78.9 3.1 fusion
  82.0 3.6 fusion.2
  85.6 0.5 fusion.20
  86.1 1.6 copy-done.3
  87.7 1.7 fusion.22
  89.4 1.5 pad_maximum_fusion
  91.2 7.0 %fusion.41 = f32[256,512]{1,0:T(8,128)S(1)} fusion(bf16[256,8192]{1,0:T(8,128)(2,1)} %copy-done.3, bf16[8192,512]{1,0:T(8,128)(2,1)} %param.11), kind=kOutput, calls=%fused_computation.77 | convolution fusion | flops 2147483648 | bytes 13107200 | tf_op jit(solution)/shard_map/dot_general | solution.py:117
  98.2 34.2 %all-gather.6.cloned.1.call-done = bf16[256,8192]{1,0:T(8,128)(2,1)} async-done(((bf16[256,512]{1,0:T(8,128)(2,1)}), bf16[256,8192]{1,0:T(8,128)(2,1)}) %all-gather.6.cloned.1.call-update) | async-done | bytes 4194320 | tf_op jit(solution)/shard_map/all_gather | solution.py:132
  132.4 7.0 %convolution_convert_fusion = bf16[256,512]{1,0:T(8,128)(2,1)S(1)} fusion(bf16[256,8192]{1,0:T(8,128)(2,1)} %all-gather.6.cloned.1.call-done, bf16[512,8192]{1,0:T(8,128)(2,1)} %param.14), kind=kOutput, calls=%fused_computation.24 | convolution fusion | flops 2147614720 | bytes 12845056 | tf_op jit(solution)/shard_map/dot_general | solution.py:133
  139.8 0.3 fusion.39
  140.3 4.6 %multiply_reduce_fusion = (f32[4,256]{1,0:T(4,128)S(1)}, f32[4,256,2048]{2,1,0:T(8,128)}) fusion(bf16[2048,1,256]{2,0,1:T(8,128)(2,1)S(1)} %bitcast.97, bf16[256,4,64]{2,0,1:T(8,128)(2,1)S(1)} %get-tuple-element.21, bf16[256,4,64]{2,0,1:T(8,128)(2,1)S(1)} %get-tuple-element.20), kind=kOutput, calls=%fused_computation.7 | convolution fusion | flops 541588480 | bytes 9441280 | tf_op jit(solution)/shard_map/gtd,cd->gtc/dot_general | solution.py:32
  144.8 87.2 %all-reduce.2.cloned.1.call-done = f32[256,2048]{1,0:T(8,128)} async-done(((f32[256,2048]{1,0:T(8,128)}), f32[256,2048]{1,0:T(8,128)}) %all-reduce.2.cloned.1.call-update) | async-done | bytes 2097168 | tf_op jit(solution)/shard_map/psum | solution.py:101
  232.0 1.5 slice_bitcast_fusion
  233.7 0.4 subtract_convert_fusion
  234.1 0.3 pad_maximum_fusion.2
  234.6 0.8 copy-done.4
  235.3 0.4 fusion.40
  235.9 1.9 fusion.4
  237.8 1.3 slice.63
  239.1 0.8 copy-done.5
  239.9 0.3 fusion.18
  240.3 2.3 multiply_reduce_fusion.1
  242.6 0.9 slice-done.1
  243.5 5.8 %fusion.42 = f32[256,8192]{1,0:T(8,128)} fusion(bf16[256,512]{0,1:T(8,128)(2,1)S(1)} %bitcast.107, bf16[512,8192]{1,0:T(8,128)(2,1)S(1)} %bitcast.95), kind=kOutput, calls=%fused_computation.78 | convolution fusion | flops 2147483648 | bytes 17039360 | tf_op jit(solution)/shard_map/dot_general | solution.py:143
  249.3 5.6 %convolution_bitcast_fusion = f32[2048,128]{0,1:T(8,128)} fusion(bf16[4,256,128]{1,2,0:T(8,128)(2,1)S(1)} %bitcast.108, f32[4,256,2048]{2,1,0:T(8,128)} %get-tuple-element.31, f32[4,256]{1,0:T(4,128)S(1)} %add.115, f32[4,256]{1,0:T(4,128)S(1)} %max.8), kind=kOutput, calls=%fused_computation.10 | convolution fusion | flops 545259520 | bytes 9707520 | tf_op jit(solution)/shard_map/gtc,gtd->cd/dot_general | solution.py:68
  254.9 8.5 %fusion.5 = f32[2048,128]{0,1:T(8,128)} fusion(bf16[4,256,128]{1,2,0:T(8,128)(2,1)S(1)} %bitcast.109, f32[4,256]{1,0:T(4,128)S(1)} %get-tuple-element.34, bf16[2048,1,256]{2,0,1:T(8,128)(2,1)S(1)} %bitcast.99, bf16[256,4,64]{2,0,1:T(8,128)(2,1)S(1)} %get-tuple-element.21, bf16[256,4,64]{2,0,1:T(8,128)(2,1)S(1)} %get-tuple-element.20, ...), kind=kOutput, calls=%fused_computation.12 | convolution fusion | flops 1087111168 | bytes 10760192 | tf_op jit(solution)/shard_map/gtc,gtd->cd/dot_general | solution.py:66
  263.4 3.4 copy_bitcast_fusion
  266.8 3.8 all-to-all-start.1
  270.6 0.9 constant_dynamic-slice_fusion.1
  271.5 0.7 copy.54
  272.2 0.9 constant_dynamic-slice_fusion
  273.2 0.7 copy.55
  273.9 64.4 %all-to-all-done.1 = f32[16,128,256]{1,2,0:T(8,128)S(1)} async-done(((f32[16,128,256]{1,2,0:T(8,128)}), f32[16,128,256]{1,2,0:T(8,128)S(1)}, u32[]{:S(2)}, u32[]{:S(2)}) %all-to-all-start.1) | async-done | bytes 2097184 | tf_op jit(solution)/shard_map/all_to_all | solution.py:151
  338.4 0.6 copy.80
  339.2 1.0 copy.53
  340.3 1.0 copy.52
  341.3 49.7 %reduce-scatter.2.cloned.1.call-done = f32[256,512]{1,0:T(8,128)} async-done(((f32[256,8192]{1,0:T(8,128)}), f32[256,512]{1,0:T(8,128)}) %reduce-scatter.2.cloned.1.call-update) | async-done | bytes 524304 | tf_op jit(solution)/shard_map/reduce_scatter | solution.py:144
  391.0 1.8 convert_element_type.74
  (39 shorter events, 2.1 us)
Async XLA Ops:
  7.2 78.4 %copy-start = (bf16[512,1024]{1,0:T(8,128)(2,1)S(1)}, bf16[512,1024]{1,0:T(8,128)(2,1)}, u32[]{:S(2)}) copy-start(bf16[512,1024]{1,0:T(8,128)(2,1)} %param.13) | copy-start | bytes 3145732
  7.2 71.7 %all-gather.4.cloned.1.call-start = ((), (), s32[]{:S(2)}) async-start(), calls=%async_computation.3 | async-start | bytes 4456448 | tf_op jit(solution)/shard_map/all_gather | solution.py:85
  7.9 124.5 %all-gather.6.cloned.1.call-start = ((), (), s32[]{:S(2)}) async-start(), calls=%async_computation.6 | async-start | bytes 4456448 | tf_op jit(solution)/shard_map/all_gather | solution.py:132
  12.0 128.3 %all-to-all-start = ((bf16[128,16,256]{2,0,1:T(8,128)(2,1)}), bf16[128,16,256]{2,0,1:T(8,128)(2,1)S(1)}, u32[]{:S(2)}, u32[]{:S(2)}) async-start(bf16[128,16,256]{2,0,1:T(8,128)(2,1)} %pad_maximum_fusion.1), calls=%async_computation | async-start | bytes 2097152 | tf_op jit(solution)/shard_map/all_to_all | solution.py:123
  19.4 212.6 %all-reduce.2.cloned.1.call-start = ((), (), s32[]{:S(2)}) async-start(), calls=%async_computation.4 | async-start | bytes 4194304 | tf_op jit(solution)/shard_map/psum | solution.py:101
  85.6 2.1 copy-start.3
  91.0 300.0 %reduce-scatter.2.cloned.1.call-start = ((), (), s32[]{:S(2)}) async-start(), calls=%async_computation.5 | async-start | bytes 8912896 | tf_op jit(solution)/shard_map/reduce_scatter | solution.py:144
  232.0 3.9 copy-start.2
  234.5 0.8 copy-start.4
  239.1 0.8 copy-start.5
  239.9 2.7 slice-start
  240.3 3.2 slice-start.1
  263.4 129.4 %copy-start.1 = (bf16[512,1024]{1,0:T(8,128)(2,1)S(1)}, bf16[512,1024]{1,0:T(8,128)(2,1)}, u32[]{:S(2)}) copy-start(bf16[512,1024]{1,0:T(8,128)(2,1)} %param.13) | copy-start | bytes 3145732
  266.8 71.4 %all-to-all-start.1 = ((f32[16,128,256]{1,2,0:T(8,128)}), f32[16,128,256]{1,2,0:T(8,128)S(1)}, u32[]{:S(2)}, u32[]{:S(2)}) async-start(f32[16,128,256]{1,2,0:T(8,128)} %copy_bitcast_fusion), calls=%async_computation.2 | async-start | bytes 4194304 | tf_op jit(solution)/shard_map/all_to_all | solution.py:151
Sparse Core Ops, SparseCore 0:
  10.2 68.6 all-gather.3
  81.0 51.3 all-gather.5
  136.0 95.9 all-reduce.1
  249.4 141.5 reduce-scatter.1
where the time goes:
time: 400 us; the launch traced here: 399 us
  waiting for transfers between devices  254 us (64%)
  matrix products  43.7 us (11%)
  blocking collectives  40.6 us (10%)
  other arithmetic  18.3 us (5%)
  local copies, waits for them, and re-layouts  16.8 us (4%)
  between operations  14.1 us (4%)
  starting transfers between devices  11.5 us (3%)
    psum x1, waiting for transfers between devices, on_device(): token_kv = lax.psum(partial_kv, 'fsdp')  87.2 us
    all_to_all x1, waiting for transfers between devices, on_device(): lax.all_to_all(stacked, 'fsdp', split_axis=0, concat_axis=0, tiled=True)  64.4 us
    reduce_scatter x1, waiting for transfers between devices, on_device(): lax.psum_scatter(partial_out, 'fsdp', scatter_dimension=1, tiled=True)  49.7 us
    all_gather x1, blocking collectives, on_device(): lax.all_gather(norm_gain, 'fsdp', axis=0, tiled=True)  40.6 us
    all_gather x1, waiting for transfers between devices, on_device(): cotangent = lax.all_gather(grad_out, 'fsdp', axis=1, tiled=True)  34.2 us
    all_gather x1, waiting for transfers between devices, on_device(): lax.all_gather(layer_input, 'fsdp', axis=1, tiled=True)  17.4 us
    unnamed x25, local copies, waits for them, and re-layouts  10.6 us
    dot_general x1, matrix products, head_block(): jnp.einsum('gtc,gtd->cd', grad_score, queries, preferred_element_type=jnp...  8.53 us
  transfers between devices with their start and end apart: 6, of which 5 were waited for; matrix products, arithmetic and copies ran while one was open for 15% of the time, Pallas kernels for 0%

commit v1 on v0

--- a/solution.py
+++ b/solution.py
@@ -1,6 +1,8 @@
 import jax
 import jax.numpy as jnp
 from jax import lax
+from jax.experimental import pallas as pl
+from jax.experimental.pallas import tpu as pltpu
 from jax.sharding import PartitionSpec as P
 
 H = 64
@@ -157,9 +159,380 @@
     return (attn_out, grad_key, grad_value, new_keys, new_values)
 
 
+BF = jnp.bfloat16
+F32 = jnp.float32
+ROWS = 128
+
+
+def dot(a, b):
+    return jnp.dot(a, b, preferred_element_type=F32)
+
+
+def dot_t(a, b):
+    return lax.dot_general(a, b, (((1,), (1,)), ((), ())), preferred_element_type=F32)
+
+
+def layer_kernel(
+    x_ref, gain_ref, cos_ref, sin_ref, wq_hbm, wk_hbm, wv_hbm, wo_hbm, ck_ref, cv_ref, go_ref,
+    out_ref, gk_ref, gv_ref, nk_ref, nv_ref,
+    normed, cot, wq, wk, wv, wo, slot_k, slot_v, squares,
+    kv_swap, kv_got, kv_send, kv_recv, tok,
+    queries, probs, heads, grads, acc, acc_got, g_send, g_recv,
+    o_swap, o_got, y_send, y_recv, z_send, z_recv,
+    load_sem, sq_send, sq_recv, cart_send, cart_recv, n_send, n_recv, c_send, c_recv,
+    kv_ssem, kv_rsem, os_send, os_recv, gr_send, gr_recv,
+):
+    me = lax.axis_index("fsdp")
+    core = lax.rem(me, 2)
+    chip = me // 2
+    ydim = lax.rem(chip, 2)
+    zdim = chip // 2
+    other = 1 - core
+
+    def device(chip_index, core_index):
+        return {"fsdp": chip_index * 2 + core_index}
+
+    def zchip(steps, yy):
+        return lax.rem(zdim + steps + 4, 4) * 2 + yy
+
+    def remote(source, target, send, recv, where):
+        return pltpu.make_async_remote_copy(
+            src_ref=source, dst_ref=target, send_sem=send, recv_sem=recv,
+            device_id=where, device_id_type=pl.DeviceIdType.MESH,
+        )
+
+    sent = []
+
+    def push(source, target, send, recv, where):
+        copy = remote(source, target, send, recv, where)
+        copy.start()
+        sent.append(copy)
+        return copy
+
+    loads = [
+        pltpu.make_async_copy(source, target, load_sem.at[index])
+        for index, (source, target) in enumerate(
+            [(wk_hbm, wk), (wv_hbm, wv), (wq_hbm, wq), (wo_hbm, wo)]
+        )
+    ]
+    for load in loads:
+        load.start()
+
+    barrier = pltpu.get_barrier_semaphore()
+    for step in range(1, 16):
+        pl.semaphore_signal(
+            barrier, inc=1, device_id={"fsdp": lax.rem(me + step, 16)},
+            device_id_type=pl.DeviceIdType.MESH,
+        )
+
+    x = x_ref[...].astype(F32)
+    own = jnp.sum(x * x, axis=1, keepdims=True)
+    squares[0] = jnp.broadcast_to(own, (256, 128)).T[:8]
+    pl.semaphore_wait(barrier, 15)
+
+    sq = [
+        push(squares.at[0], squares.at[step], sq_send.at[step - 1], sq_recv.at[step - 1],
+             {"fsdp": lax.rem(me + step, 16)})
+        for step in range(1, 16)
+    ]
+
+    cart = []
+    for step in range(1, 8):
+        there = lax.rem(chip + step, 8)
+        columns = pl.ds(pl.multiple_of(there * 128, 128), 128)
+        cart.append(push(ck_ref.at[:, columns], slot_k.at[core, chip], cart_send.at[0, step],
+                         cart_recv.at[0, step], device(there, core)))
+        cart.append(push(cv_ref.at[:, columns], slot_v.at[core, chip], cart_send.at[1, step],
+                         cart_recv.at[1, step], device(there, core)))
+    mine = pl.ds(pl.multiple_of(chip * 128, 128), 128)
+    slot_k[core, chip] = ck_ref[:, mine]
+    slot_v[core, chip] = cv_ref[:, mine]
+
+    for copy in sq:
+        copy.wait_recv()
+    total = squares[0]
+    for step in range(1, 16):
+        total = total + squares[step]
+    total = jnp.broadcast_to(total[:1], (128, 256)).T[:, :1]
+    inverse = lax.rsqrt(total * (1.0 / 8192.0) + 1e-05)
+    normed[core, chip] = (
+        x_ref[...].astype(F32) * inverse * gain_ref[...].astype(F32)
+    ).astype(BF)
+    cot[core, chip] = go_ref[...]
+
+    def gather_start(buffer, k):
+        own_slot = buffer.at[core, chip]
+        first = [
+            push(own_slot, own_slot, n_send.at[k, 0, d], n_recv.at[k, 0, d], device(zchip(d, ydim), core))
+            for d in range(1, 4)
+        ]
+        second = [push(own_slot, own_slot, n_send.at[k, 1, 0], n_recv.at[k, 1, 0], device(zdim * 2 + 1 - ydim, core))]
+        push(own_slot, own_slot, c_send.at[k, 0, 0], c_recv.at[k, 0, 0], device(chip, other))
+        return first, second
+
+    def gather_forward(buffer, k, first, second):
+        for d in range(1, 4):
+            first[d - 1].wait_recv()
+            slot = buffer.at[core, zchip(-d, ydim)]
+            second.append(push(slot, slot, n_send.at[k, 1, d], n_recv.at[k, 1, d], device(zdim * 2 + 1 - ydim, core)))
+            push(slot, slot, c_send.at[k, 0, d], c_recv.at[k, 0, d], device(chip, other))
+
+    def gather_finish(buffer, k, second):
+        for d in range(4):
+            second[d].wait_recv()
+            slot = buffer.at[core, zchip(-d, 1 - ydim)]
+            push(slot, slot, c_send.at[k, 1, d], c_recv.at[k, 1, d], device(chip, other))
+        for part in range(2):
+            for d in range(4):
+                slot = buffer.at[other, zchip(-d, ydim if part == 0 else 1 - ydim)]
+                remote(slot, slot, c_send.at[k, part, d], c_recv.at[k, part, d], device(chip, other)).wait_recv()
+
+    first_n, second_n = gather_start(normed, 0)
+
+    loads[0].wait()
+    loads[1].wait()
+
+    def partial_kv(g, tokens_of):
+        rows = pl.ds(pl.multiple_of(tokens_of * ROWS, ROWS), ROWS)
+        columns = pl.ds(pl.multiple_of(g * 128, 128), 128)
+        left = normed[core, chip, rows, :]
+        return dot(left, wk[:, columns]), dot(left, wv[:, columns])
+
+    @pl.loop(0, 8)
+    def _(g):
+        a, b = partial_kv(g, other)
+        kv_swap[g, 0] = a
+        kv_swap[g, 1] = b
+
+    swap = push(kv_swap, kv_got, kv_ssem.at[0], kv_rsem.at[0], device(chip, other))
+    gather_forward(normed, 0, first_n, second_n)
+    swap.wait_recv()
+
+    @pl.loop(0, 8)
+    def _(g):
+        a, b = partial_kv(g, core)
+        kv_send[g, 0] = a + kv_got[g, 0]
+        kv_send[g, 1] = b + kv_got[g, 1]
+
+    kv = []
+    for step in range(1, 8):
+        there = lax.rem(chip + step, 8)
+        kv.append(push(kv_send.at[there], kv_recv.at[step - 1], kv_ssem.at[step], kv_rsem.at[step], device(there, core)))
+    gather_finish(normed, 0, second_n)
+    first_g, second_g = gather_start(cot, 1)
+
+    loads[2].wait()
+
+    def project(source, weight):
+        def body(index, total):
+            cc, g = index // 8, lax.rem(index, 8)
+            rows = pl.ds(pl.multiple_of((g * 2 + cc) * 512, 512), 512)
+            return total + dot(source[cc, g], weight[rows, :])
+        return lax.fori_loop(0, 16, body, jnp.zeros((256, 512), F32))
+
+    cosines = cos_ref[...]
+    sines = sin_ref[...]
+
+    def rotated(v, c, s):
+        return v * c + pltpu.roll(v, 64, 1) * s
+
+    cos2 = jnp.concatenate([cosines, cosines], 0)
+    sin2 = jnp.concatenate([sines, sines], 0)
+    q_all = project(normed, wq)
+    for h in range(4):
+        queries[h] = rotated(q_all[:, h * 128:(h + 1) * 128], cos2, sin2).astype(BF)
+
+    for copy in cart:
+        copy.wait_recv()
+    swap_k = push(slot_k.at[core], slot_k.at[core], cart_send.at[0, 0], cart_recv.at[0, 0], device(chip, other))
+    swap_v = push(slot_v.at[core], slot_v.at[core], cart_send.at[1, 0], cart_recv.at[1, 0], device(chip, other))
+    for copy in kv:
+        copy.wait_recv()
+    key_sum = kv_send[chip, 0]
+    value_sum = kv_send[chip, 1]
+    for step in range(7):
+        key_sum = key_sum + kv_recv[step, 0]
+        value_sum = value_sum + kv_recv[step, 1]
+    tok[core, 0] = rotated(key_sum, cosines, sines).astype(BF)
+    tok[core, 1] = value_sum.astype(BF)
+    swap_t = push(tok.at[core], tok.at[core], kv_ssem.at[8], kv_rsem.at[8], device(chip, other))
+    gather_forward(cot, 1, first_g, second_g)
+    swap_t.wait_recv()
+    for half in range(2):
+        rows = slice(half * ROWS, (half + 1) * ROWS)
+        for which, target in ((0, nk_ref), (1, nv_ref)):
+            block = tok[half, which].astype(F32)
+            target[rows, :] = jnp.where(core == 0, block[:, :64], block[:, 64:]).astype(BF)
+    swap_k.wait_recv()
+    swap_v.wait_recv()
+
+    scaling = HD ** (-0.5)
+    token_row = lax.broadcasted_iota(jnp.int32, (ROWS, ROWS), 0)
+    token_col = lax.broadcasted_iota(jnp.int32, (ROWS, ROWS), 1)
+    causal = (token_row // SEQ == token_col // SEQ) & (token_col <= token_row)
+
+    @pl.loop(0, 8)
+    def _(index):
+        h, half = index // 2, lax.rem(index, 2)
+        rows = pl.ds(pl.multiple_of(half * ROWS, ROWS), ROWS)
+        q = queries[h, rows, :]
+        keys = slot_k[...].reshape(C, HD)
+        score = dot_t(q, keys) * scaling
+        score_tok = jnp.where(causal, dot_t(q, tok[half, 0]) * scaling, -jnp.inf)
+        top = jnp.maximum(
+            jnp.max(score, -1, keepdims=True), jnp.max(score_tok, -1, keepdims=True)
+        )
+        e = jnp.exp(score - top)
+        e_tok = jnp.exp(score_tok - top)
+        inv = 1.0 / (jnp.sum(e, -1, keepdims=True) + jnp.sum(e_tok, -1, keepdims=True))
+        p = e * inv
+        probs[h, rows, :] = p
+        mixture = dot(p.astype(BF), slot_v[...].reshape(C, HD))
+        mixture = mixture + dot((e_tok * inv).astype(BF), tok[half, 1])
+        heads[h, rows, :] = mixture.astype(BF)
+
+    gather_finish(cot, 1, second_g)
+
+    loads[3].wait()
+    all_heads = jnp.concatenate([heads[h] for h in range(4)], 1)
+
+    def partial_out(g, cc):
+        columns = pl.ds(pl.multiple_of((g * 2 + cc) * 512, 512), 512)
+        return dot(all_heads, wo[:, columns])
+
+    swaps = []
+    for index, (d, yy) in enumerate([(d, k) for k in (1, 0) for d in (1, 2, 3, 0)]):
+        g = zchip(d, 1 - ydim if yy else ydim)
+        o_swap[index] = partial_out(g, other)
+        swaps.append(push(o_swap.at[index], o_got.at[index], os_send.at[0, index], os_recv.at[0, index], device(chip, other)))
+    ys = []
+    for index, d in enumerate((1, 2, 3, 0)):
+        part = partial_out(zchip(d, 1 - ydim), core)
+        swaps[index].wait_recv()
+        y_send[index] = (part + o_got[index]).astype(BF)
+        ys.append(push(y_send.at[index], y_recv.at[index], os_send.at[1, index], os_recv.at[1, index], device(zdim * 2 + 1 - ydim, core)))
+
+    def grad_body(index, total):
+        cc, g = index // 8, lax.rem(index, 8)
+        columns = pl.ds(pl.multiple_of((g * 2 + cc) * 512, 512), 512)
+        return total + dot_t(cot[cc, g], wo[:, columns])
+
+    g_all = lax.fori_loop(0, 16, grad_body, jnp.zeros((256, 512), F32)).astype(BF)
+    for h in range(4):
+        grads[h] = g_all[:, h * 128:(h + 1) * 128]
+
+    zs = []
+    for index, d in enumerate((1, 2, 3)):
+        part = partial_out(zchip(d, ydim), core)
+        swaps[4 + index].wait_recv()
+        ys[index].wait_recv()
+        z_send[index] = (part + o_got[4 + index] + y_recv[index].astype(F32)).astype(BF)
+        zs.append(push(z_send.at[index], z_recv.at[index], os_send.at[2, index], os_recv.at[2, index], device(zchip(d, ydim), core)))
+
+    acc[...] = jnp.zeros_like(acc)
+
+    @pl.loop(0, 8)
+    def _(index):
+        h, half = index // 2, lax.rem(index, 2)
+        rows = pl.ds(pl.multiple_of(half * ROWS, ROWS), ROWS)
+        q_t = queries[h, rows, :].T
+        gh = grads[h, rows, :]
+        gh_t = gh.T
+        delta = jnp.sum(gh.astype(F32) * heads[h, rows, :].astype(F32), -1, keepdims=True)
+        for cc in range(2):
+            values = slot_v[cc].reshape(C // 2, HD)
+            p = probs[h, rows, cc * (C // 2):(cc + 1) * (C // 2)]
+            score = (p * (dot_t(gh, values) - delta)).astype(BF)
+            acc[cc, 0] += dot(q_t, score)
+            acc[cc, 1] += dot(gh_t, p.astype(BF))
+
+    swap_a = push(acc.at[other], acc_got, gr_send.at[0], gr_recv.at[0], device(chip, other))
+
+    part = partial_out(chip, core)
+    swaps[7].wait_recv()
+    ys[3].wait_recv()
+    part = part + o_got[7] + y_recv[3].astype(F32)
+    for index in range(3):
+        zs[index].wait_recv()
+        part = part + z_recv[index].astype(F32)
+    out_ref[...] = part.astype(BF)
+
+    swap_a.wait_recv()
+    for which in range(2):
+        both = acc[core, which] + acc_got[which]
+        if which == 0:
+            both = both * scaling
+        for g in range(8):
+            g_send[g, which] = both[:, g * 128:(g + 1) * 128].astype(BF)
+    gs = []
+    for step in range(1, 8):
+        there = lax.rem(chip + step, 8)
+        gs.append(push(g_send.at[there], g_recv.at[step - 1], gr_send.at[step], gr_recv.at[step], device(there, core)))
+
+    gk_ref[:, mine] = g_send[chip, 0].astype(F32).T
+    gv_ref[:, mine] = g_send[chip, 1].astype(F32).T
+    for step in range(1, 8):
+        gs[step - 1].wait_recv()
+        columns = pl.ds(pl.multiple_of(lax.rem(chip - step + 8, 8) * 128, 128), 128)
+        gk_ref[:, columns] = g_recv[step - 1, 0].astype(F32).T
+        gv_ref[:, columns] = g_recv[step - 1, 1].astype(F32).T
+    for copy in sent:
+        copy.wait_send()
+
+
+def on_chip_grid(
+    layer_input, norm_gain, w_query, w_key, w_value, w_out, cart_key, cart_value, grad_out
+):
+    half = HD // 2
+    frequency = jnp.exp(-jnp.log(500000.0) * jnp.arange(half, dtype=F32) * (2.0 / HD))
+    positions = C + jnp.arange(ROWS) % SEQ
+    angles = positions.astype(F32)[:, None] * frequency[None, :]
+    cosines = jnp.concatenate([jnp.cos(angles), jnp.cos(angles)], 1)
+    sines = jnp.concatenate([-jnp.sin(angles), jnp.sin(angles)], 1)
+    vmem = pl.BlockSpec(memory_space=pltpu.VMEM)
+    hbm = pl.BlockSpec(memory_space=pl.ANY)
+    V = pltpu.VMEM
+    dma = pltpu.SemaphoreType.DMA
+    return tuple(pl.pallas_call(
+        layer_kernel,
+        out_shape=(
+            jax.ShapeDtypeStruct((256, 512), BF),
+            jax.ShapeDtypeStruct((128, 1024), F32),
+            jax.ShapeDtypeStruct((128, 1024), F32),
+            jax.ShapeDtypeStruct((256, 64), BF),
+            jax.ShapeDtypeStruct((256, 64), BF),
+        ),
+        in_specs=[vmem, vmem, vmem, vmem, hbm, hbm, hbm, hbm, vmem, vmem, vmem],
+        out_specs=(vmem,) * 5,
+        scratch_shapes=[
+            V((2, 8, 256, 512), BF), V((2, 8, 256, 512), BF),
+            V((8192, 512), BF), V((512, 1024), BF), V((512, 1024), BF), V((512, 8192), BF),
+            V((2, 8, 128, 128), BF), V((2, 8, 128, 128), BF), V((16, 8, 256), F32),
+            V((8, 2, 128, 128), F32), V((8, 2, 128, 128), F32), V((8, 2, 128, 128), F32),
+            V((7, 2, 128, 128), F32), V((2, 2, 128, 128), BF),
+            V((4, 256, 128), BF), V((4, 256, 2048), F32), V((4, 256, 128), BF), V((4, 256, 128), BF),
+            V((2, 2, 128, 1024), F32), V((2, 128, 1024), F32),
+            V((8, 2, 128, 128), BF), V((7, 2, 128, 128), BF),
+            V((8, 256, 512), F32), V((8, 256, 512), F32),
+            V((4, 256, 512), BF), V((4, 256, 512), BF), V((3, 256, 512), BF), V((3, 256, 512), BF),
+            dma((4,)), dma((15,)), dma((15,)), dma((2, 8)), dma((2, 8)),
+            dma((2, 2, 4)), dma((2, 2, 4)), dma((2, 2, 4)), dma((2, 2, 4)),
+            dma((9,)), dma((9,)), dma((3, 8)), dma((3, 8)), dma((8,)), dma((8,)),
+        ],
+        compiler_params=pltpu.CompilerParams(
+            collective_id=0, has_side_effects=True, vmem_limit_bytes=63 * 2**20
+        ),
+        name="attention_layer",
+    )(
+        layer_input, norm_gain.reshape(1, -1), cosines, sines, w_query, w_key, w_value, w_out,
+        cart_key, cart_value, grad_out,
+    ))
+
+
 def solution(mesh):
+    body = on_chip_grid if mesh.shape["fsdp"] == 16 else on_device
     return jax.shard_map(
-        on_device,
+        body,
         mesh=mesh,
         in_specs=(
             P("groups", "fsdp"),

time: 400 us -> 171 us (0.43)
  waiting for transfers between devices: 254 us -> 0 us
  Pallas kernels: 0 us -> 159 us
  matrix products: 43.7 us -> 0 us
  blocking collectives: 40.6 us -> 0 us
  other arithmetic: 18.3 us -> 1.08 us
  between operations: 14.1 us -> 0.66 us
  starting transfers between devices: 11.5 us -> 0 us
  local copies, waits for them, and re-layouts: 16.8 us -> 9.78 us
    pallas_call x0 -> x1, Pallas kernels: none -> 159 us  [on_chip_grid(): pl.pallas_call(layer_kernel, out_shape=(jax.ShapeDtypeStruct((256, 512),...]
    psum x1 -> x0, waiting for transfers between devices: 87.2 us -> none  [on_device(): token_kv = lax.psum(partial_kv, 'fsdp')]
    all_to_all x2 -> x0, waiting for transfers between devices: 64.4 us -> none  [the longest x1 64.4 us: on_device(): lax.all_to_all(stacked, 'fsdp', split_axis=0, concat_axis=0, tiled=True)]
    all_gather x2 -> x0, waiting for transfers between devices: 51.6 us -> none  [the longest x1 34.2 us: on_device(): cotangent = lax.all_gather(grad_out, 'fsdp', axis=1, tiled=True)]
    reduce_scatter x1 -> x0, waiting for transfers between devices: 49.7 us -> none  [on_device(): lax.psum_scatter(partial_out, 'fsdp', scatter_dimension=1, tiled=True)]
    dot_general x11 -> x0, matrix products: 43.7 us -> none  [the longest x1 8.53 us: head_block(): jnp.einsum('gtc,gtd->cd', grad_score, queries, preferred_element_type=jnp...]
    all_gather x1 -> x0, blocking collectives: 40.6 us -> none  [on_device(): lax.all_gather(norm_gain, 'fsdp', axis=0, tiled=True)]
    all_to_all x2 -> x0, starting transfers between devices: 11.2 us -> none  [the longest x1 7.39 us: on_device(): lax.all_to_all(jnp.concatenate([spread_keys, spread_values], 2), 'fsdp',...]
  transfers between devices with their start and end apart: 6 -> 0, of which waited for: 5 -> 0; matrix products, arithmetic and copies ran while one was open for 15% -> 0% of each run, Pallas kernels for 0% -> 0%
where the time goes in v1:
time: 171 us; the launch traced here: 170 us
  Pallas kernels  159 us (93%)
  local copies, waits for them, and re-layouts  9.78 us (6%)
    pallas_call x1, Pallas kernels, on_chip_grid(): pl.pallas_call(layer_kernel, out_shape=(jax.ShapeDtypeStruct((256, 512),...  159 us
    unnamed x3, local copies, waits for them, and re-layouts  5.44 us

profile of v1, /device:TPU:0, one launch (start us, length us, event | category | flops | bytes accessed | tf_op | source)
XLA Modules:
  0.0 170.4 jit_solution(1838928546673014061)
XLA Ops:
  0.7 1.3 reshape.29.gain_ref
  1.9 0.3 fusion
  2.2 0.8 pad_maximum_fusion
  3.0 158.9 %attention_layer.1 = (bf16[256,512]{1,0:T(8,128)(2,1)}, f32[128,1024]{1,0:T(8,128)}, f32[128,1024]{1,0:T(8,128)}, bf16[256,64]{1,0:T(8,128)(2,1)}, bf16[256,64]{1,0:T(8,128)(2,1)}) custom-call(bf16[256,512]{1,0:T(8,128)(2,1)} %x_ref.1, bf16[1,512]{1,0:T(2,128)(2,1)} %reshape.29.gain_ref, f32[128,128]{1,0:T(8,128)} %get-tuple-element.13.cos_ref, ...), custom_call_target="tpu_custom_call" | custom-call | tf_op jit(solution)/shard_map/attention_layer/pallas_call | solution.py:496
  161.9 1.5 copy.14
  163.4 1.5 copy.15
  164.9 1.7 copy.19
  166.6 1.9 %copy.20 = f32[128,1024]{1,0:T(8,128)} copy(f32[128,1024]{1,0:T(8,128)} %get-tuple-element.21) | data formatting | bytes 1048576
  168.5 1.9 %copy.21 = f32[128,1024]{1,0:T(8,128)} copy(f32[128,1024]{1,0:T(8,128)} %get-tuple-element.22) | data formatting | bytes 1048576
  (2 shorter events, 0.0 us)

commit v2 on v1

--- a/solution.py
+++ b/solution.py
@@ -176,10 +176,10 @@
     x_ref, gain_ref, cos_ref, sin_ref, wq_hbm, wk_hbm, wv_hbm, wo_hbm, ck_ref, cv_ref, go_ref,
     out_ref, gk_ref, gv_ref, nk_ref, nv_ref,
     normed, cot, wq, wk, wv, wo, slot_k, slot_v, squares,
-    kv_swap, kv_got, kv_send, kv_recv, tok,
+    kv_swap, kv_got, kv_send, kv_y, kv_z, kv_recv, tok,
     queries, probs, heads, grads, acc, acc_got, g_send, g_recv,
     o_swap, o_got, y_send, y_recv, z_send, z_recv,
-    load_sem, sq_send, sq_recv, cart_send, cart_recv, n_send, n_recv, c_send, c_recv,
+    load_sem, sq_send, sq_recv, cart_send, cart_recv, n_send, n_recv, yg_send, yg_recv, c_send, c_recv,
     kv_ssem, kv_rsem, os_send, os_recv, gr_send, gr_recv,
 ):
     me = lax.axis_index("fsdp")
@@ -203,10 +203,16 @@
 
     sent = []
 
-    def push(source, target, send, recv, where):
+    def guarded(valid, action):
+        if valid is None:
+            action()
+        else:
+            pl.when(valid)(action)
+
+    def push(source, target, send, recv, where, valid=None):
         copy = remote(source, target, send, recv, where)
-        copy.start()
-        sent.append(copy)
+        guarded(valid, copy.start)
+        sent.append((valid, copy))
         return copy
 
     loads = [
@@ -260,34 +266,58 @@
     ).astype(BF)
     cot[core, chip] = go_ref[...]
 
+    above = device(zchip(1, ydim), core)
+    below = device(zchip(-1, ydim), core)
+    across = device(zdim * 2 + 1 - ydim, core)
+    twin = device(chip, other)
+
+    def arrivals(step):
+        return (
+            (0, -1 - step, zdim >= 1 + step, (zdim >= 1 + step) & (zdim < 3), above),
+            (1, 1 + step, zdim < 3 - step, (zdim < 3 - step) & (zdim > 0), below),
+        )
+
     def gather_start(buffer, k):
-        own_slot = buffer.at[core, chip]
-        first = [
-            push(own_slot, own_slot, n_send.at[k, 0, d], n_recv.at[k, 0, d], device(zchip(d, ydim), core))
-            for d in range(1, 4)
-        ]
-        second = [push(own_slot, own_slot, n_send.at[k, 1, 0], n_recv.at[k, 1, 0], device(zdim * 2 + 1 - ydim, core))]
-        push(own_slot, own_slot, c_send.at[k, 0, 0], c_recv.at[k, 0, 0], device(chip, other))
-        return first, second
-
-    def gather_forward(buffer, k, first, second):
-        for d in range(1, 4):
-            first[d - 1].wait_recv()
-            slot = buffer.at[core, zchip(-d, ydim)]
-            second.append(push(slot, slot, n_send.at[k, 1, d], n_recv.at[k, 1, d], device(zdim * 2 + 1 - ydim, core)))
-            push(slot, slot, c_send.at[k, 0, d], c_recv.at[k, 0, d], device(chip, other))
-
-    def gather_finish(buffer, k, second):
-        for d in range(4):
-            second[d].wait_recv()
-            slot = buffer.at[core, zchip(-d, 1 - ydim)]
-            push(slot, slot, c_send.at[k, 1, d], c_recv.at[k, 1, d], device(chip, other))
-        for part in range(2):
-            for d in range(4):
-                slot = buffer.at[other, zchip(-d, ydim if part == 0 else 1 - ydim)]
-                remote(slot, slot, c_send.at[k, part, d], c_recv.at[k, part, d], device(chip, other)).wait_recv()
-
-    first_n, second_n = gather_start(normed, 0)
+        slot = buffer.at[core, chip]
+        push(slot, slot, n_send.at[k, 0, 0], n_recv.at[k, 0, 0], above, zdim < 3)
+        push(slot, slot, n_send.at[k, 1, 0], n_recv.at[k, 1, 0], below, zdim > 0)
+        push(slot, slot, yg_send.at[k, 6], yg_recv.at[k, 6], across)
+        push(slot, slot, c_send.at[k, 0, 6], c_recv.at[k, 0, 6], twin)
+
+    def gather_step(buffer, k, step):
+        for way, offset, here, further, onward in arrivals(step):
+            slot = buffer.at[core, zchip(offset, ydim)]
+            number = way * 3 + step
+            arrived = remote(slot, slot, n_send.at[k, way, step], n_recv.at[k, way, step], onward)
+            guarded(here, arrived.wait_recv)
+            if step < 2:
+                push(slot, slot, n_send.at[k, way, step + 1], n_recv.at[k, way, step + 1], onward, further)
+            push(slot, slot, yg_send.at[k, number], yg_recv.at[k, number], across, here)
+            push(slot, slot, c_send.at[k, 0, number], c_recv.at[k, 0, number], twin, here)
+
+    def gather_across(buffer, k, steps):
+        for step in steps:
+            pairs = [(6, 0, None)] if step < 0 else [
+                (way * 3 + step, offset, here) for way, offset, here, _, _ in arrivals(step)
+            ]
+            for number, offset, here in pairs:
+                slot = buffer.at[core, zchip(offset, 1 - ydim)]
+                arrived = remote(slot, slot, yg_send.at[k, number], yg_recv.at[k, number], across)
+                guarded(here, arrived.wait_recv)
+                push(slot, slot, c_send.at[k, 1, number], c_recv.at[k, 1, number], twin, here)
+
+    def gather_finish(buffer, k):
+        for step in (-1, 0, 1, 2):
+            pairs = [(6, 0, None)] if step < 0 else [
+                (way * 3 + step, offset, here) for way, offset, here, _, _ in arrivals(step)
+            ]
+            for number, offset, here in pairs:
+                for part in range(2):
+                    slot = buffer.at[other, zchip(offset, ydim if part == 0 else 1 - ydim)]
+                    arrived = remote(slot, slot, c_send.at[k, part, number], c_recv.at[k, part, number], twin)
+                    guarded(here, arrived.wait_recv)
+
+    gather_start(normed, 0)
 
     loads[0].wait()
     loads[1].wait()
@@ -305,21 +335,30 @@
         kv_swap[g, 1] = b
 
     swap = push(kv_swap, kv_got, kv_ssem.at[0], kv_rsem.at[0], device(chip, other))
-    gather_forward(normed, 0, first_n, second_n)
+    gather_step(normed, 0, 0)
     swap.wait_recv()
 
     @pl.loop(0, 8)
     def _(g):
         a, b = partial_kv(g, core)
-        kv_send[g, 0] = a + kv_got[g, 0]
-        kv_send[g, 1] = b + kv_got[g, 1]
-
+        yy, zz = lax.rem(g, 2), g // 2
+        kv_send[yy, zz, 0] = a + kv_got[g, 0]
+        kv_send[yy, zz, 1] = b + kv_got[g, 1]
+
+    kv_across = push(kv_send.at[1 - ydim], kv_y, kv_ssem.at[1], kv_rsem.at[1], across)
+    gather_step(normed, 0, 1)
+    gather_across(normed, 0, (-1, 0))
+    kv_across.wait_recv()
     kv = []
-    for step in range(1, 8):
-        there = lax.rem(chip + step, 8)
-        kv.append(push(kv_send.at[there], kv_recv.at[step - 1], kv_ssem.at[step], kv_rsem.at[step], device(there, core)))
-    gather_finish(normed, 0, second_n)
-    first_g, second_g = gather_start(cot, 1)
+    for d in (1, 2, 3, 0):
+        zz = lax.rem(zdim + d, 4)
+        kv_z[d] = kv_send[ydim, zz] + kv_y[zz]
+        if d:
+            kv.append(push(kv_z.at[d], kv_recv.at[d - 1], kv_ssem.at[1 + d], kv_rsem.at[1 + d], device(zchip(d, ydim), core)))
+    gather_step(normed, 0, 2)
+    gather_start(cot, 1)
+    gather_across(normed, 0, (1, 2))
+    gather_finish(normed, 0)
 
     loads[2].wait()
 
@@ -348,21 +387,21 @@
     swap_v = push(slot_v.at[core], slot_v.at[core], cart_send.at[1, 0], cart_recv.at[1, 0], device(chip, other))
     for copy in kv:
         copy.wait_recv()
-    key_sum = kv_send[chip, 0]
-    value_sum = kv_send[chip, 1]
-    for step in range(7):
+    key_sum = kv_z[0, 0]
+    value_sum = kv_z[0, 1]
+    for step in range(3):
         key_sum = key_sum + kv_recv[step, 0]
         value_sum = value_sum + kv_recv[step, 1]
     tok[core, 0] = rotated(key_sum, cosines, sines).astype(BF)
     tok[core, 1] = value_sum.astype(BF)
     swap_t = push(tok.at[core], tok.at[core], kv_ssem.at[8], kv_rsem.at[8], device(chip, other))
-    gather_forward(cot, 1, first_g, second_g)
+    gather_step(cot, 1, 0)
     swap_t.wait_recv()
     for half in range(2):
-        rows = slice(half * ROWS, (half + 1) * ROWS)
+        tokens = slice(half * ROWS, (half + 1) * ROWS)
         for which, target in ((0, nk_ref), (1, nv_ref)):
-            block = tok[half, which].astype(F32)
-            target[rows, :] = jnp.where(core == 0, block[:, :64], block[:, 64:]).astype(BF)
+            block = tok[half, which].astype(F32).T
+            target[:, tokens] = jnp.where(core == 0, block[:64], block[64:]).astype(BF)
     swap_k.wait_recv()
     swap_v.wait_recv()
 
@@ -371,8 +410,7 @@
     token_col = lax.broadcasted_iota(jnp.int32, (ROWS, ROWS), 1)
     causal = (token_row // SEQ == token_col // SEQ) & (token_col <= token_row)
 
-    @pl.loop(0, 8)
-    def _(index):
+    def attend(index):
         h, half = index // 2, lax.rem(index, 2)
         rows = pl.ds(pl.multiple_of(half * ROWS, ROWS), ROWS)
         q = queries[h, rows, :]
@@ -391,7 +429,14 @@
         mixture = mixture + dot((e_tok * inv).astype(BF), tok[half, 1])
         heads[h, rows, :] = mixture.astype(BF)
 
-    gather_finish(cot, 1, second_g)
+    pl.loop(0, 2)(attend)
+    gather_step(cot, 1, 1)
+    pl.loop(2, 4)(attend)
+    gather_step(cot, 1, 2)
+    pl.loop(4, 6)(attend)
+    gather_across(cot, 1, (-1, 0))
+    pl.loop(6, 8)(attend)
+    gather_across(cot, 1, (1, 2))
 
     loads[3].wait()
     all_heads = jnp.concatenate([heads[h] for h in range(4)], 1)
@@ -411,6 +456,8 @@
         swaps[index].wait_recv()
         y_send[index] = (part + o_got[index]).astype(BF)
         ys.append(push(y_send.at[index], y_recv.at[index], os_send.at[1, index], os_recv.at[1, index], device(zdim * 2 + 1 - ydim, core)))
+
+    gather_finish(cot, 1)
 
     def grad_body(index, total):
         cc, g = index // 8, lax.rem(index, 8)
@@ -476,8 +523,20 @@
         columns = pl.ds(pl.multiple_of(lax.rem(chip - step + 8, 8) * 128, 128), 128)
         gk_ref[:, columns] = g_recv[step - 1, 0].astype(F32).T
         gv_ref[:, columns] = g_recv[step - 1, 1].astype(F32).T
-    for copy in sent:
-        copy.wait_send()
+    for valid, copy in sent:
+        guarded(valid, copy.wait_send)
+
+
+def place_kernel(*refs):
+    sources, targets, sems = refs[:5], refs[5:10], refs[10]
+    copies = [
+        pltpu.make_async_copy(source, target, sems.at[index])
+        for index, (source, target) in enumerate(zip(sources, targets))
+    ]
+    for copy in copies:
+        copy.start()
+    for copy in copies:
+        copy.wait()
 
 
 def on_chip_grid(
@@ -493,30 +552,32 @@
     hbm = pl.BlockSpec(memory_space=pl.ANY)
     V = pltpu.VMEM
     dma = pltpu.SemaphoreType.DMA
-    return tuple(pl.pallas_call(
+    shapes = (
+        jax.ShapeDtypeStruct((256, 512), BF),
+        jax.ShapeDtypeStruct((128, 1024), F32),
+        jax.ShapeDtypeStruct((128, 1024), F32),
+        jax.ShapeDtypeStruct((64, 256), BF),
+        jax.ShapeDtypeStruct((64, 256), BF),
+    )
+    results = pl.pallas_call(
         layer_kernel,
-        out_shape=(
-            jax.ShapeDtypeStruct((256, 512), BF),
-            jax.ShapeDtypeStruct((128, 1024), F32),
-            jax.ShapeDtypeStruct((128, 1024), F32),
-            jax.ShapeDtypeStruct((256, 64), BF),
-            jax.ShapeDtypeStruct((256, 64), BF),
-        ),
+        out_shape=shapes,
         in_specs=[vmem, vmem, vmem, vmem, hbm, hbm, hbm, hbm, vmem, vmem, vmem],
         out_specs=(vmem,) * 5,
         scratch_shapes=[
             V((2, 8, 256, 512), BF), V((2, 8, 256, 512), BF),
             V((8192, 512), BF), V((512, 1024), BF), V((512, 1024), BF), V((512, 8192), BF),
             V((2, 8, 128, 128), BF), V((2, 8, 128, 128), BF), V((16, 8, 256), F32),
-            V((8, 2, 128, 128), F32), V((8, 2, 128, 128), F32), V((8, 2, 128, 128), F32),
-            V((7, 2, 128, 128), F32), V((2, 2, 128, 128), BF),
+            V((8, 2, 128, 128), F32), V((8, 2, 128, 128), F32), V((2, 4, 2, 128, 128), F32),
+            V((4, 2, 128, 128), F32), V((4, 2, 128, 128), F32), V((3, 2, 128, 128), F32),
+            V((2, 2, 128, 128), BF),
             V((4, 256, 128), BF), V((4, 256, 2048), F32), V((4, 256, 128), BF), V((4, 256, 128), BF),
             V((2, 2, 128, 1024), F32), V((2, 128, 1024), F32),
             V((8, 2, 128, 128), BF), V((7, 2, 128, 128), BF),
             V((8, 256, 512), F32), V((8, 256, 512), F32),
             V((4, 256, 512), BF), V((4, 256, 512), BF), V((3, 256, 512), BF), V((3, 256, 512), BF),
             dma((4,)), dma((15,)), dma((15,)), dma((2, 8)), dma((2, 8)),
-            dma((2, 2, 4)), dma((2, 2, 4)), dma((2, 2, 4)), dma((2, 2, 4)),
+            dma((2, 2, 3)), dma((2, 2, 3)), dma((2, 7)), dma((2, 7)), dma((2, 2, 7)), dma((2, 2, 7)),
             dma((9,)), dma((9,)), dma((3, 8)), dma((3, 8)), dma((8,)), dma((8,)),
         ],
         compiler_params=pltpu.CompilerParams(
@@ -526,7 +587,16 @@
     )(
         layer_input, norm_gain.reshape(1, -1), cosines, sines, w_query, w_key, w_value, w_out,
         cart_key, cart_value, grad_out,
-    ))
+    )
+    attn_out, grad_key, grad_value, keys_t, values_t = pl.pallas_call(
+        place_kernel,
+        out_shape=shapes,
+        in_specs=[hbm] * 5,
+        out_specs=(hbm,) * 5,
+        scratch_shapes=[dma((5,))],
+        name="place_results",
+    )(*results)
+    return attn_out, grad_key, grad_value, keys_t.T, values_t.T
 
 
 def solution(mesh):

time: 171 us -> 185 us (1.082)
  Pallas kernels: 159 us -> 181 us
  local copies, waits for them, and re-layouts: 9.78 us -> 1.26 us
    pallas_call x1 -> x2, Pallas kernels: 159 us -> 181 us  [the longest x1 138 us: on_chip_grid(): pl.pallas_call(layer_kernel, out_shape=shapes, in_specs=[vmem, vmem, vmem...]
    unnamed x3 -> x0, local copies, waits for them, and re-layouts: 5.44 us -> none
    pallas_call x2 -> x0, local copies, waits for them, and re-layouts: 3.08 us -> none  [on_chip_grid(): pl.pallas_call(layer_kernel, out_shape=(jax.ShapeDtypeStruct((256, 512),...]
where the time goes in v2:
time: 185 us; the launch traced here: 184 us
  Pallas kernels  181 us (98%)
    pallas_call x1, Pallas kernels, on_chip_grid(): pl.pallas_call(layer_kernel, out_shape=shapes, in_specs=[vmem, vmem, vmem...  138 us
    pallas_call x1, Pallas kernels, on_chip_grid(): pl.pallas_call(place_kernel, out_shape=shapes, in_specs=[hbm] * 5, out_sp...  42.8 us

profile of v2, /device:TPU:0, one launch (start us, length us, event | category | flops | bytes accessed | tf_op | source)
XLA Modules:
  0.0 184.1 jit_solution(749853614526448310)
XLA Ops:
  0.7 1.3 reshape.29.gain_ref
  1.9 0.3 fusion
  2.2 0.8 pad_maximum_fusion
  3.0 138.2 %attention_layer.1 = (bf16[256,512]{1,0:T(8,128)(2,1)}, f32[128,1024]{1,0:T(8,128)}, f32[128,1024]{1,0:T(8,128)}, bf16[64,256]{1,0:T(8,128)(2,1)}, bf16[64,256]{1,0:T(8,128)(2,1)}) custom-call(bf16[256,512]{1,0:T(8,128)(2,1)} %x_ref.1, bf16[1,512]{1,0:T(2,128)(2,1)} %reshape.29.gain_ref, f32[128,128]{1,0:T(8,128)} %get-tuple-element.28.cos_ref, ...), custom_call_target="tpu_custom_call" | custom-call | tf_op jit(solution)/shard_map/attention_layer/pallas_call | solution.py:562
  141.2 42.8 %place_results.1 = (bf16[256,512]{1,0:T(8,128)(2,1)}, f32[128,1024]{1,0:T(8,128)}, f32[128,1024]{1,0:T(8,128)}, bf16[64,256]{1,0:T(8,128)(2,1)}, bf16[64,256]{1,0:T(8,128)(2,1)}) custom-call(bf16[256,512]{1,0:T(8,128)(2,1)} %get-tuple-element.15.refs_0_, f32[128,1024]{1,0:T(8,128)} %get-tuple-element.16.refs_1_, f32[128,1024]{1,0:T(8,128)} %get-tuple-element.17.refs_2_, ...), custom_call_target="tpu_custom_call" | custom-call | tf_op jit(solution)/shard_map/place_results/pallas_call | solution.py:591
  (2 shorter events, 0.0 us)

commit v3 on v2

--- a/solution.py
+++ b/solution.py
@@ -347,7 +347,10 @@
 
     kv_across = push(kv_send.at[1 - ydim], kv_y, kv_ssem.at[1], kv_rsem.at[1], across)
     gather_step(normed, 0, 1)
-    gather_across(normed, 0, (-1, 0))
+    gather_across(normed, 0, (-1,))
+    gather_step(normed, 0, 2)
+    gather_start(cot, 1)
+    gather_across(normed, 0, (0,))
     kv_across.wait_recv()
     kv = []
     for d in (1, 2, 3, 0):
@@ -355,9 +358,9 @@
         kv_z[d] = kv_send[ydim, zz] + kv_y[zz]
         if d:
             kv.append(push(kv_z.at[d], kv_recv.at[d - 1], kv_ssem.at[1 + d], kv_rsem.at[1 + d], device(zchip(d, ydim), core)))
-    gather_step(normed, 0, 2)
-    gather_start(cot, 1)
-    gather_across(normed, 0, (1, 2))
+    gather_across(normed, 0, (1,))
+    gather_step(cot, 1, 0)
+    gather_across(normed, 0, (2,))
     gather_finish(normed, 0)
 
     loads[2].wait()
@@ -381,6 +384,7 @@
     for h in range(4):
         queries[h] = rotated(q_all[:, h * 128:(h + 1) * 128], cos2, sin2).astype(BF)
 
+    gather_step(cot, 1, 1)
     for copy in cart:
         copy.wait_recv()
     swap_k = push(slot_k.at[core], slot_k.at[core], cart_send.at[0, 0], cart_recv.at[0, 0], device(chip, other))
@@ -395,7 +399,7 @@
     tok[core, 0] = rotated(key_sum, cosines, sines).astype(BF)
     tok[core, 1] = value_sum.astype(BF)
     swap_t = push(tok.at[core], tok.at[core], kv_ssem.at[8], kv_rsem.at[8], device(chip, other))
-    gather_step(cot, 1, 0)
+    gather_step(cot, 1, 2)
     swap_t.wait_recv()
     for half in range(2):
         tokens = slice(half * ROWS, (half + 1) * ROWS)
@@ -429,14 +433,9 @@
         mixture = mixture + dot((e_tok * inv).astype(BF), tok[half, 1])
         heads[h, rows, :] = mixture.astype(BF)
 
-    pl.loop(0, 2)(attend)
-    gather_step(cot, 1, 1)
-    pl.loop(2, 4)(attend)
-    gather_step(cot, 1, 2)
-    pl.loop(4, 6)(attend)
+    pl.loop(0, 4)(attend)
     gather_across(cot, 1, (-1, 0))
-    pl.loop(6, 8)(attend)
-    gather_across(cot, 1, (1, 2))
+    pl.loop(4, 8)(attend)
 
     loads[3].wait()
     all_heads = jnp.concatenate([heads[h] for h in range(4)], 1)
@@ -457,6 +456,7 @@
         y_send[index] = (part + o_got[index]).astype(BF)
         ys.append(push(y_send.at[index], y_recv.at[index], os_send.at[1, index], os_recv.at[1, index], device(zdim * 2 + 1 - ydim, core)))
 
+    gather_across(cot, 1, (1, 2))
     gather_finish(cot, 1)
 
     def grad_body(index, total):
@@ -468,18 +468,9 @@
     for h in range(4):
         grads[h] = g_all[:, h * 128:(h + 1) * 128]
 
-    zs = []
-    for index, d in enumerate((1, 2, 3)):
-        part = partial_out(zchip(d, ydim), core)
-        swaps[4 + index].wait_recv()
-        ys[index].wait_recv()
-        z_send[index] = (part + o_got[4 + index] + y_recv[index].astype(F32)).astype(BF)
-        zs.append(push(z_send.at[index], z_recv.at[index], os_send.at[2, index], os_recv.at[2, index], device(zchip(d, ydim), core)))
-
     acc[...] = jnp.zeros_like(acc)
 
-    @pl.loop(0, 8)
-    def _(index):
+    def differentiate(index):
         h, half = index // 2, lax.rem(index, 2)
         rows = pl.ds(pl.multiple_of(half * ROWS, ROWS), ROWS)
         q_t = queries[h, rows, :].T
@@ -493,16 +484,17 @@
             acc[cc, 0] += dot(q_t, score)
             acc[cc, 1] += dot(gh_t, p.astype(BF))
 
+    zs = []
+    for index, d in enumerate((1, 2, 3)):
+        pl.loop(2 * index, 2 * index + 2)(differentiate)
+        part = partial_out(zchip(d, ydim), core)
+        swaps[4 + index].wait_recv()
+        ys[index].wait_recv()
+        z_send[index] = (part + o_got[4 + index] + y_recv[index].astype(F32)).astype(BF)
+        zs.append(push(z_send.at[index], z_recv.at[index], os_send.at[2, index], os_recv.at[2, index], device(zchip(d, ydim), core)))
+    pl.loop(6, 8)(differentiate)
+
     swap_a = push(acc.at[other], acc_got, gr_send.at[0], gr_recv.at[0], device(chip, other))
-
-    part = partial_out(chip, core)
-    swaps[7].wait_recv()
-    ys[3].wait_recv()
-    part = part + o_got[7] + y_recv[3].astype(F32)
-    for index in range(3):
-        zs[index].wait_recv()
-        part = part + z_recv[index].astype(F32)
-    out_ref[...] = part.astype(BF)
 
     swap_a.wait_recv()
     for which in range(2):
@@ -516,6 +508,15 @@
         there = lax.rem(chip + step, 8)
         gs.append(push(g_send.at[there], g_recv.at[step - 1], gr_send.at[step], gr_recv.at[step], device(there, core)))
 
+    part = partial_out(chip, core)
+    swaps[7].wait_recv()
+    ys[3].wait_recv()
+    part = part + o_got[7] + y_recv[3].astype(F32)
+    for index in range(3):
+        zs[index].wait_recv()
+        part = part + z_recv[index].astype(F32)
+    out_ref[...] = part.astype(BF)
+
     gk_ref[:, mine] = g_send[chip, 0].astype(F32).T
     gv_ref[:, mine] = g_send[chip, 1].astype(F32).T
     for step in range(1, 8):
@@ -528,15 +529,8 @@
 
 
 def place_kernel(*refs):
-    sources, targets, sems = refs[:5], refs[5:10], refs[10]
-    copies = [
-        pltpu.make_async_copy(source, target, sems.at[index])
-        for index, (source, target) in enumerate(zip(sources, targets))
-    ]
-    for copy in copies:
-        copy.start()
-    for copy in copies:
-        copy.wait()
+    for source, target in zip(refs[:5], refs[5:]):
+        target[...] = source[...]
 
 
 def on_chip_grid(
@@ -591,9 +585,8 @@
     attn_out, grad_key, grad_value, keys_t, values_t = pl.pallas_call(
         place_kernel,
         out_shape=shapes,
-        in_specs=[hbm] * 5,
-        out_specs=(hbm,) * 5,
-        scratch_shapes=[dma((5,))],
+        in_specs=[vmem] * 5,
+        out_specs=(vmem,) * 5,
         name="place_results",
     )(*results)
     return attn_out, grad_key, grad_value, keys_t.T, values_t.T

time: 185 us -> 140 us (0.76)
  Pallas kernels: 181 us -> 136 us
    pallas_call x1, Pallas kernels: 42.8 us -> 2.4 us  [on_chip_grid(): pl.pallas_call(place_kernel, out_shape=shapes, in_specs=[vmem] * 5, out_s...]
    pallas_call x1, Pallas kernels: 138 us -> 133 us  [on_chip_grid(): pl.pallas_call(layer_kernel, out_shape=shapes, in_specs=[vmem, vmem, vmem...]
where the time goes in v3:
time: 140 us; the launch traced here: 139 us
  Pallas kernels  136 us (97%)
    pallas_call x1, Pallas kernels, on_chip_grid(): pl.pallas_call(layer_kernel, out_shape=shapes, in_specs=[vmem, vmem, vmem...  133 us

profile of v3, /device:TPU:0, one launch (start us, length us, event | category | flops | bytes accessed | tf_op | source)
XLA Modules:
  0.0 138.5 jit_solution(4715507616273118129)
XLA Ops:
  0.7 1.3 reshape.29.gain_ref
  1.9 0.3 fusion
  2.2 0.8 pad_maximum_fusion
  3.0 133.1 %attention_layer.1 = (bf16[256,512]{1,0:T(8,128)(2,1)}, f32[128,1024]{1,0:T(8,128)}, f32[128,1024]{1,0:T(8,128)}, bf16[64,256]{1,0:T(8,128)(2,1)}, bf16[64,256]{1,0:T(8,128)(2,1)}) custom-call(bf16[256,512]{1,0:T(8,128)(2,1)} %x_ref.1, bf16[1,512]{1,0:T(2,128)(2,1)} %reshape.29.gain_ref, f32[128,128]{1,0:T(8,128)} %get-tuple-element.28.cos_ref, ...), custom_call_target="tpu_custom_call" | custom-call | tf_op jit(solution)/shard_map/attention_layer/pallas_call | solution.py:556
  136.1 2.4 %place_results.1 = (bf16[256,512]{1,0:T(8,128)(2,1)}, f32[128,1024]{1,0:T(8,128)}, f32[128,1024]{1,0:T(8,128)}, bf16[64,256]{1,0:T(8,128)(2,1)}, bf16[64,256]{1,0:T(8,128)(2,1)}) custom-call(bf16[256,512]{1,0:T(8,128)(2,1)} %get-tuple-element.15.refs_0_, f32[128,1024]{1,0:T(8,128)} %get-tuple-element.16.refs_1_, f32[128,1024]{1,0:T(8,128)} %get-tuple-element.17.refs_2_, ...), custom_call_target="tpu_custom_call" | custom-call | tf_op jit(solution)/shard_map/place_results/pallas_call | solution.py:585
  (2 shorter events, 0.0 us)
